TPU v7x, 512 devices: a whole 4x8x8 slice. The times are simulated.
512 devices in a mesh: wave: 4 (over y_hi, core), tx: 8 (over z), ty: 16 (over x, y_lo).
Axes of the slice: x: 4, y: 8 (y_hi: 2, y_lo: 4; y = y_hi * 4 + y_lo), z: 8, core: 2. Of those that a mesh axis runs over, the one named last changes fastest.
Arguments:
- initial_fields: float32 [4, 2, 12, 128, 8192], P('wave', None, None, 'tx', 'ty'), may hold values from -6 to 6
- source_profiles: float32 [4, 2, 3, 8192], P('wave'), may hold values from -6 to 6
- source_waveforms: float32 [4, 2, 5], P('wave'), may hold values from -3 to 3
- material_map: int32 [128, 8192], P('tx', 'ty'), may hold values from 0 to 2
- design_density: float32 [128, 8192], P('tx', 'ty'), may hold values from 0 to 1
- material_table: float32 [3, 4], replicated, may hold values from 0.02 to 12, as said below
- plane_indices: int32 [2], replicated, may hold values from 0 to 127
- design_box: int32 [6], replicated, may hold values from 0 to 128, as said below
Outputs:
- density_gradient: float32 [128, 8192], P('tx', 'ty')
- final_electric: float32 [4, 2, 3, 128, 8192], P('wave', None, None, 'tx', 'ty')
Inputs may be any that keep to these rules, and one draw needn't show every extreme that they name: `material_map`: material ids are below 3. `material_table`: column 0 lies in [1, 12], column 1 in [0.5, 3], column 2 in [0.3, 1.5], column 3 in [0.02, 0.5]. `plane_indices`: entry 0 is the source plane of the forward run, entry 1 the monitor plane where the adjoint run's source enters. `design_box`: x0 <= 16, y0 <= 16, x1 = 128, y1 = 128, z0 = 0, z1 = 64.
All inputs are finite; a program needn't handle non-finite values.
Results may differ from a plain program's by a relative error of at most 0.0001.
Values sent between devices are 32-bit elements; how exact they have to be, the bound alone decides.
A program may use at most 64 MiB of HBM per device.

v0:
```python
import jax
import jax.numpy as jnp
from jax import lax
from jax.sharding import PartitionSpec as P

NZ = 64
STEPS = 5
NMAT = 3
time_step = 0.5
contrast = 2.0


def shifted_2(value, axis, steps):
    count = lax.axis_size(axis)
    initial, last = (max(0, -steps), min(count, count - steps))
    return lax.ppermute(value, axis, [(source, source + steps) for source in range(initial, last)])


def ahead_rows(values, border):
    return jnp.concatenate([values[:, 1:], border], axis=1)


def behind_rows(values, border):
    return jnp.concatenate([border, values[:, :-1]], axis=1)


def ahead_lines(values, border):
    width = border.shape[2]
    return jnp.concatenate([values[:, :, width:], border], axis=2)


def behind_lines(values, border):
    width = border.shape[2]
    return jnp.concatenate([border, values[:, :, :-width]], axis=2)


def ahead_depth(values, depth_last):
    shifted = jnp.concatenate([values[:, :, 1:], jnp.zeros_like(values[:, :, :1])], axis=2)
    return jnp.where(depth_last, 0.0, shifted)


def behind_depth(values, depth_first):
    shifted = jnp.concatenate([jnp.zeros_like(values[:, :, :1]), values[:, :, :-1]], axis=2)
    return jnp.where(depth_first, 0.0, shifted)


def curl_electric(field, rows_ahead, lines_ahead, depth_last):
    part_one, part_two, part_three = (field[:, 0], field[:, 1], field[:, 2])
    curl_one = (
        ahead_lines(part_three, lines_ahead[:, 1])
        - part_three
        - (ahead_depth(part_two, depth_last) - part_two)
    )
    curl_two = (
        ahead_depth(part_one, depth_last)
        - part_one
        - (ahead_rows(part_three, rows_ahead[:, 1]) - part_three)
    )
    curl_three = (
        ahead_rows(part_two, rows_ahead[:, 0])
        - part_two
        - (ahead_lines(part_one, lines_ahead[:, 0]) - part_one)
    )
    return jnp.stack([curl_one, curl_two, curl_three], axis=1)


def curl_magnetic(field, rows_behind, lines_behind, depth_first):
    part_one, part_two, part_three = (field[:, 0], field[:, 1], field[:, 2])
    curl_one = (
        part_three
        - behind_lines(part_three, lines_behind[:, 1])
        - (part_two - behind_depth(part_two, depth_first))
    )
    curl_two = (
        part_one
        - behind_depth(part_one, depth_first)
        - (part_three - behind_rows(part_three, rows_behind[:, 1]))
    )
    curl_three = (
        part_two
        - behind_rows(part_two, rows_behind[:, 0])
        - (part_one - behind_lines(part_one, lines_behind[:, 0]))
    )
    return jnp.stack([curl_one, curl_two, curl_three], axis=1)


def electric_borders(field):
    rows_ahead = shifted_2(field[:, 1:, :1, :], "tx", -1)
    flat_part = field[:, 0::2, :, :NZ].reshape(field.shape[0], 2, field.shape[2] * NZ)
    lines_ahead = shifted_2(flat_part, "ty", -1)
    return (rows_ahead, lines_ahead.reshape(field.shape[0], 2, field.shape[2], NZ))


def magnetic_borders(field):
    rows_behind = shifted_2(field[:, 1:, -1:, :], "tx", 1)
    flat_part = field[:, 0::2, :, -NZ:].reshape(field.shape[0], 2, field.shape[2] * NZ)
    lines_behind = shifted_2(flat_part, "ty", 1)
    return (rows_behind, lines_behind.reshape(field.shape[0], 2, field.shape[2], NZ))


def design_mask(grid_rows, grid_flat, design_box):
    lines = grid_flat // NZ
    depth_ids = grid_flat % NZ
    in_rows = (grid_rows >= design_box[0]) & (grid_rows < design_box[1])
    in_lines = (
        (lines >= design_box[2])
        & (lines < design_box[3])
        & (depth_ids >= design_box[4])
        & (depth_ids < design_box[5])
    )
    return (in_rows[:, None] & in_lines[None, :]).astype(jnp.float32)


def coefficients(material_map, design_density, material_table, inside_design):
    damping = material_table[:, 3]
    denom = 1.0 + 0.25 * damping
    decay = (1.0 - 0.25 * damping) / denom
    drive = material_table[:, 2] * material_table[:, 2] * time_step / denom
    coupled = drive * material_table[:, 1]
    permittivity = jnp.zeros(material_map.shape, jnp.float32)
    decay_map = jnp.zeros(material_map.shape, jnp.float32)
    drive_map = jnp.zeros(material_map.shape, jnp.float32)
    coupled_map = jnp.zeros(material_map.shape, jnp.float32)
    for material_id in range(NMAT):
        chosen = (material_map == material_id).astype(jnp.float32)
        permittivity = permittivity + chosen * material_table[material_id, 0]
        decay_map = decay_map + chosen * decay[material_id]
        drive_map = drive_map + chosen * drive[material_id]
        coupled_map = coupled_map + chosen * coupled[material_id]
    permittivity = permittivity + inside_design * design_density * contrast
    return jnp.stack([time_step / permittivity, decay_map, drive_map, coupled_map])


def advance(
    electric,
    magnetic,
    polarization,
    current,
    coeffs,
    inside,
    depth_last,
    depth_first,
    source,
    get_electric,
    get_magnetic,
):
    rows_ahead, lines_ahead = get_electric(electric)
    magnetic = (
        magnetic - time_step * curl_electric(electric, rows_ahead, lines_ahead, depth_last)
    ) * inside
    current = coeffs[1] * current + coeffs[3] * electric - coeffs[2] * polarization
    polarization = polarization + time_step * current
    rows_behind, lines_behind = get_magnetic(magnetic)
    electric = electric + coeffs[0] * (
        curl_magnetic(magnetic, rows_behind, lines_behind, depth_first) - current - source
    )
    return (electric, magnetic, polarization, current)


def on_device(
    initial_fields,
    source_profiles,
    source_waveforms,
    material_map,
    design_density,
    material_table,
    plane_indices,
    design_box,
):
    rows_here, flat_here = material_map.shape
    tile_row = lax.axis_index("tx")
    tile_col = lax.axis_index("ty")
    grid_rows = tile_row * rows_here + jnp.arange(rows_here, dtype=jnp.int32)
    grid_flat = tile_col * flat_here + jnp.arange(flat_here, dtype=jnp.int32)
    inside_design = design_mask(grid_rows, grid_flat, design_box)
    coeffs = coefficients(material_map, design_density, material_table, inside_design)
    fields = initial_fields[0]
    profiles = source_profiles[0]
    waveforms = source_waveforms[0]
    inside = 1.0
    profiles_here = lax.dynamic_slice_in_dim(profiles, tile_col * flat_here, flat_here, axis=2)
    depth_ids = grid_flat % NZ
    depth_last = depth_ids == NZ - 1
    depth_first = depth_ids == 0
    plane_rows = (grid_rows[None, :] == plane_indices[:, None]).astype(jnp.float32)
    electric = fields[:, 0:3]
    magnetic = fields[:, 3:6]
    polarization = fields[:, 6:9]
    current = fields[:, 9:12]
    forward_history = [electric[0]]
    adjoint_history = [electric[1]]
    for step_index in range(STEPS):
        source = (
            waveforms[:, step_index][:, None, None, None]
            * profiles_here[:, :, None, :]
            * plane_rows[:, None, :, None]
        )
        electric, magnetic, polarization, current = advance(
            electric,
            magnetic,
            polarization,
            current,
            coeffs,
            inside,
            depth_last,
            depth_first,
            source,
            electric_borders,
            magnetic_borders,
        )
        forward_history.append(electric[0])
        adjoint_history.append(electric[1])
    partial_value = jnp.zeros((rows_here, flat_here), jnp.float32)
    for pair_index in range(1, STEPS + 1):
        partial_value = partial_value + jnp.sum(
            adjoint_history[STEPS + 1 - pair_index]
            * (forward_history[pair_index] - forward_history[pair_index - 1]),
            axis=0,
        )
    collected = lax.psum(partial_value, "wave")
    density_gradient = contrast * inside_design * collected
    return (density_gradient, electric[None])


def solution(mesh):
    placed = (
        P("wave", None, None, "tx", "ty"),
        P("wave", None, None, None),
        P("wave", None, None),
        P("tx", "ty"),
        P("tx", "ty"),
        P(),
        P(),
        P(),
    )
    return jax.shard_map(
        on_device,
        mesh=mesh,
        in_specs=placed,
        out_specs=(P("tx", "ty"), P("wave", None, None, "tx", "ty")),
        check_vma=False,
    )
```

profile of v0, /device:TPU:212, one launch (start us, length us, event | category | flops | bytes accessed | tf_op | source)
XLA Modules:
  0.0 151.3 jit_solution(15769013824842356531)
XLA Ops:
  0.6 1.2 copy.212
  2.0 2.4 %collective-permute-start = (f32[2,2,1024]{2,0,1:T(2,128)S(1)}, f32[2,2,1024]{2,0,1:T(2,128)S(1)}, u32[]{:S(2)}, u32[]{:S(2)}) collective-permute-start(f32[2,2,1024]{2,0,1:T(2,128)S(1)} %reshape.295), channel_id=1, source_target_pairs={{1,0},{2,1},{3,2},{4,3},{5,4},{6,5},{7,6},{8,7},{9,8},{10,9},{11,1... | collective-permute-start | bytes 49160 | tf_op jit(solution)/shard_map/ppermute | solution.py:16
  4.3 1.9 %collective-permute-start.1 = (f32[2,2,1,512]{3,2,0,1:T(1,128)S(1)}, f32[2,2,1,512]{3,2,0,1:T(1,128)S(1)}, u32[]{:S(2)}, u32[]{:S(2)}) collective-permute-start(f32[2,2,1,512]{3,2,0,1:T(1,128)S(1)} %slice.789), channel_id=1, source_target_pairs={{16,0},{32,16},{48,32},{64,48},{80,64},{96,80},{112,96},{17,1},{33... | collective-permute-start | bytes 24584 | tf_op jit(solution)/shard_map/ppermute | solution.py:16
  9.9 1.2 compare_and_fusion.1
  11.8 2.5 %compare_and_fusion = pred[512]{0:T(512)(128)(4,1)S(1)} fusion(s32[]{:T(128)} %bitcast.5, s32[]{:T(128)} %bitcast.4, s32[]{:T(128)} %bitcast.3, s32[]{:T(128)} %bitcast.2, s32[]{:T(128)S(6)} %mul.416), kind=kLoop, calls=%fused_computation.258 | loop fusion | flops 13824 | bytes 532 | tf_op jit(solution)/shard_map/and | solution.py:106
  14.9 1.9 %fusion.80 = (f32[16,512]{1,0:T(8,128)S(1)}, pred[16,512]{1,0:T(8,128)(4,1)S(1)}, pred[16,512]{1,0:T(8,128)(4,1)S(1)}, pred[16,512]{1,0:T(8,128)(4,1)S(1)}) fusion(f32[16,512]{1,0:T(8,128)S(1)} %copy-done.9, f32[]{:T(128)} %bitcast.9, f32[]{:T(128)} %bitcast.8, f32[]{:T(128)} %bitcast.7, pred[512]{0:T(512)(128)(4,1)S(1)} %compare_and_fusion, ...), kind=kLoop, calls=%fused_computation.208 | loop fusion | flops 106496 | bytes 123420 | tf_op jit(solution)/shard_map/div | solution.py:131
  16.9 0.8 bitcast_multiply_fusion
  17.7 5.7 %select_add_fusion.2 = (f32[16,512]{1,0:T(8,128)S(1)}, f32[16,512]{1,0:T(8,128)S(1)}, f32[16,512]{1,0:T(8,128)S(1)}) fusion(pred[16,512]{1,0:T(8,128)(4,1)S(1)} %get-tuple-element.20, pred[16,512]{1,0:T(8,128)(4,1)S(1)} %get-tuple-element.19, pred[16,512]{1,0:T(8,128)(4,1)S(1)} %get-tuple-element.18, f32[]{:T(128)} %bitcast.30, f32[]{:T(128)} %bitcast.29, ...), kind=kLoop, calls=%fused_computation.212 | loop fusion | flops 122880 | bytes 122916 | tf_op jit(solution)/shard_map/add | solution.py:127
  24.3 3.5 %collective-permute-start.2 = (f32[2,2,1024]{2,0,1:T(2,128)S(1)}, f32[2,2,1024]{2,0,1:T(2,128)S(1)}, u32[]{:S(2)}, u32[]{:S(2)}) collective-permute-start(f32[2,2,1024]{2,0,1:T(2,128)S(1)} %reshape.297), channel_id=1, source_target_pairs={{0,1},{1,2},{2,3},{3,4},{4,5},{5,6},{6,7},{7,8},{8,9},{9,10},{10,1... | collective-permute-start | bytes 49160 | tf_op jit(solution)/shard_map/ppermute | solution.py:16
  27.8 5.5 %collective-permute-start.3 = (f32[2,2,1,512]{3,2,0,1:T(1,128)S(1)}, f32[2,2,1,512]{3,2,0,1:T(1,128)S(1)}, u32[]{:S(2)}, u32[]{:S(2)}) collective-permute-start(f32[2,2,1,512]{3,2,0,1:T(1,128)S(1)} %slice.802), channel_id=1, source_target_pairs={{0,16},{16,32},{32,48},{48,64},{64,80},{80,96},{96,112},{1,17},{17... | collective-permute-start | bytes 24584 | tf_op jit(solution)/shard_map/ppermute | solution.py:16
  33.3 1.3 collective-permute-done.3
  35.2 1.9 %collective-permute-start.5 = (f32[2,2,1,512]{3,1,2,0:T(2,128)S(1)}, f32[2,2,1,512]{3,1,2,0:T(2,128)S(1)}, u32[]{:S(2)}, u32[]{:S(2)}) collective-permute-start(f32[2,2,1,512]{3,1,2,0:T(2,128)S(1)} %copy.139), channel_id=1, source_target_pairs={{16,0},{32,16},{48,32},{64,48},{80,64},{96,80},{112,96},{17,1},{33... | collective-permute-start | bytes 24584 | tf_op jit(solution)/shard_map/ppermute | solution.py:16
  37.5 2.4 %collective-permute-start.4 = (f32[2,2,1024]{2,0,1:T(2,128)S(1)}, f32[2,2,1024]{2,0,1:T(2,128)S(1)}, u32[]{:S(2)}, u32[]{:S(2)}) collective-permute-start(f32[2,2,1024]{2,0,1:T(2,128)S(1)} %copy.82), channel_id=1, source_target_pairs={{1,0},{2,1},{3,2},{4,3},{5,4},{6,5},{7,6},{8,7},{9,8},{10,9},{11,1... | collective-permute-start | bytes 49160 | tf_op jit(solution)/shard_map/ppermute | solution.py:16
  39.8 2.4 %collective-permute-done.5 = f32[2,2,1,512]{3,1,2,0:T(2,128)S(1)} collective-permute-done((f32[2,2,1,512]{3,1,2,0:T(2,128)S(1)}, f32[2,2,1,512]{3,1,2,0:T(2,128)S(1)}, u32[]{:S(2)}, u32[]{:S(2)}) %collective-permute-start.5) | collective-permute-done | bytes 8224 | tf_op jit(solution)/shard_map/ppermute | solution.py:16
  42.3 3.1 %collective-permute-done.4 = f32[2,2,1024]{2,0,1:T(2,128)S(1)} collective-permute-done((f32[2,2,1024]{2,0,1:T(2,128)S(1)}, f32[2,2,1024]{2,0,1:T(2,128)S(1)}, u32[]{:S(2)}, u32[]{:S(2)}) %collective-permute-start.4) | collective-permute-done | bytes 16416 | tf_op jit(solution)/shard_map/ppermute | solution.py:16
  46.0 6.7 %collective-permute-start.6 = (f32[2,2,1024]{2,0,1:T(2,128)S(1)}, f32[2,2,1024]{2,0,1:T(2,128)S(1)}, u32[]{:S(2)}, u32[]{:S(2)}) collective-permute-start(f32[2,2,1024]{2,0,1:T(2,128)S(1)} %reshape.301), channel_id=1, source_target_pairs={{0,1},{1,2},{2,3},{3,4},{4,5},{5,6},{6,7},{7,8},{8,9},{9,10},{10,1... | collective-permute-start | bytes 49160 | tf_op jit(solution)/shard_map/ppermute | solution.py:16
  52.7 5.4 %collective-permute-start.7 = (f32[2,2,1,512]{3,2,0,1:T(1,128)S(1)}, f32[2,2,1,512]{3,2,0,1:T(1,128)S(1)}, u32[]{:S(2)}, u32[]{:S(2)}) collective-permute-start(f32[2,2,1,512]{3,2,0,1:T(1,128)S(1)} %slice.832), channel_id=1, source_target_pairs={{0,16},{16,32},{32,48},{48,64},{64,80},{80,96},{96,112},{1,17},{17... | collective-permute-start | bytes 24584 | tf_op jit(solution)/shard_map/ppermute | solution.py:16
  58.1 1.3 collective-permute-done.7
  60.1 1.9 %collective-permute-start.9 = (f32[2,2,1,512]{3,2,0,1:T(1,128)S(1)}, f32[2,2,1,512]{3,2,0,1:T(1,128)S(1)}, u32[]{:S(2)}, u32[]{:S(2)}) collective-permute-start(f32[2,2,1,512]{3,2,0,1:T(1,128)S(1)} %slice.847), channel_id=1, source_target_pairs={{16,0},{32,16},{48,32},{64,48},{80,64},{96,80},{112,96},{17,1},{33... | collective-permute-start | bytes 24584 | tf_op jit(solution)/shard_map/ppermute | solution.py:16
  62.4 1.9 %collective-permute-start.8 = (f32[2,2,1024]{2,0,1:T(2,128)S(1)}, f32[2,2,1024]{2,0,1:T(2,128)S(1)}, u32[]{:S(2)}, u32[]{:S(2)}) collective-permute-start(f32[2,2,1024]{2,0,1:T(2,128)S(1)} %copy.95), channel_id=1, source_target_pairs={{1,0},{2,1},{3,2},{4,3},{5,4},{6,5},{7,6},{8,7},{9,8},{10,9},{11,1... | collective-permute-start | bytes 49160 | tf_op jit(solution)/shard_map/ppermute | solution.py:16
  64.3 2.8 %collective-permute-done.9 = f32[2,2,1,512]{3,2,0,1:T(1,128)S(1)} collective-permute-done((f32[2,2,1,512]{3,2,0,1:T(1,128)S(1)}, f32[2,2,1,512]{3,2,0,1:T(1,128)S(1)}, u32[]{:S(2)}, u32[]{:S(2)}) %collective-permute-start.9) | collective-permute-done | bytes 8224 | tf_op jit(solution)/shard_map/ppermute | solution.py:16
  67.1 0.9 collective-permute-done.8
  68.7 4.6 %collective-permute-start.10 = (f32[2,2,1024]{2,0,1:T(2,128)S(1)}, f32[2,2,1024]{2,0,1:T(2,128)S(1)}, u32[]{:S(2)}, u32[]{:S(2)}) collective-permute-start(f32[2,2,1024]{2,0,1:T(2,128)S(1)} %reshape.305), channel_id=1, source_target_pairs={{0,1},{1,2},{2,3},{3,4},{4,5},{5,6},{6,7},{7,8},{8,9},{9,10},{10,1... | collective-permute-start | bytes 49160 | tf_op jit(solution)/shard_map/ppermute | solution.py:16
  73.3 5.4 %collective-permute-start.11 = (f32[2,2,1,512]{3,2,0,1:T(1,128)S(1)}, f32[2,2,1,512]{3,2,0,1:T(1,128)S(1)}, u32[]{:S(2)}, u32[]{:S(2)}) collective-permute-start(f32[2,2,1,512]{3,2,0,1:T(1,128)S(1)} %slice.860), channel_id=1, source_target_pairs={{0,16},{16,32},{32,48},{48,64},{64,80},{80,96},{96,112},{1,17},{17... | collective-permute-start | bytes 24584 | tf_op jit(solution)/shard_map/ppermute | solution.py:16
  78.7 1.3 collective-permute-done.11
  80.6 1.9 %collective-permute-start.13 = (f32[2,2,1,512]{3,1,2,0:T(2,128)S(1)}, f32[2,2,1,512]{3,1,2,0:T(2,128)S(1)}, u32[]{:S(2)}, u32[]{:S(2)}) collective-permute-start(f32[2,2,1,512]{3,1,2,0:T(2,128)S(1)} %copy.143), channel_id=1, source_target_pairs={{16,0},{32,16},{48,32},{64,48},{80,64},{96,80},{112,96},{17,1},{33... | collective-permute-start | bytes 24584 | tf_op jit(solution)/shard_map/ppermute | solution.py:16
  83.0 1.9 %collective-permute-start.12 = (f32[2,2,1024]{2,0,1:T(2,128)S(1)}, f32[2,2,1024]{2,0,1:T(2,128)S(1)}, u32[]{:S(2)}, u32[]{:S(2)}) collective-permute-start(f32[2,2,1024]{2,0,1:T(2,128)S(1)} %copy.107), channel_id=1, source_target_pairs={{1,0},{2,1},{3,2},{4,3},{5,4},{6,5},{7,6},{8,7},{9,8},{10,9},{11,1... | collective-permute-start | bytes 49160 | tf_op jit(solution)/shard_map/ppermute | solution.py:16
  84.9 2.7 %collective-permute-done.13 = f32[2,2,1,512]{3,1,2,0:T(2,128)S(1)} collective-permute-done((f32[2,2,1,512]{3,1,2,0:T(2,128)S(1)}, f32[2,2,1,512]{3,1,2,0:T(2,128)S(1)}, u32[]{:S(2)}, u32[]{:S(2)}) %collective-permute-start.13) | collective-permute-done | bytes 8224 | tf_op jit(solution)/shard_map/ppermute | solution.py:16
  87.6 1.0 collective-permute-done.12
  89.8 4.6 %collective-permute-start.14 = (f32[2,2,1024]{2,0,1:T(2,128)S(1)}, f32[2,2,1024]{2,0,1:T(2,128)S(1)}, u32[]{:S(2)}, u32[]{:S(2)}) collective-permute-start(f32[2,2,1024]{2,0,1:T(2,128)S(1)} %reshape.309), channel_id=1, source_target_pairs={{0,1},{1,2},{2,3},{3,4},{4,5},{5,6},{6,7},{7,8},{8,9},{9,10},{10,1... | collective-permute-start | bytes 49160 | tf_op jit(solution)/shard_map/ppermute | solution.py:16
  94.5 5.4 %collective-permute-start.15 = (f32[2,2,1,512]{3,2,0,1:T(1,128)S(1)}, f32[2,2,1,512]{3,2,0,1:T(1,128)S(1)}, u32[]{:S(2)}, u32[]{:S(2)}) collective-permute-start(f32[2,2,1,512]{3,2,0,1:T(1,128)S(1)} %slice.888), channel_id=1, source_target_pairs={{0,16},{16,32},{32,48},{48,64},{64,80},{80,96},{96,112},{1,17},{17... | collective-permute-start | bytes 24584 | tf_op jit(solution)/shard_map/ppermute | solution.py:16
  99.9 1.3 collective-permute-done.15
  103.0 0.7 slice_bitcast_fusion.4
  103.7 1.9 %collective-permute-start.17 = (f32[2,2,1,512]{3,2,0,1:T(1,128)}, f32[2,2,1,512]{3,2,0,1:T(1,128)}, u32[]{:S(2)}, u32[]{:S(2)}) collective-permute-start(f32[2,2,1,512]{3,2,0,1:T(1,128)} %slice.903), channel_id=1, source_target_pairs={{16,0},{32,16},{48,32},{64,48},{80,64},{96,80},{112,96},{17,1},{33... | collective-permute-start | bytes 24584 | tf_op jit(solution)/shard_map/ppermute | solution.py:16
  106.8 0.7 slice.899
  107.5 0.7 slice.901
  108.2 0.8 reshape.311
  109.1 1.9 %collective-permute-start.16 = (f32[2,2,1024]{2,0,1:T(2,128)S(1)}, f32[2,2,1024]{2,0,1:T(2,128)S(1)}, u32[]{:S(2)}, u32[]{:S(2)}) collective-permute-start(f32[2,2,1024]{2,0,1:T(2,128)S(1)} %copy.120), channel_id=1, source_target_pairs={{1,0},{2,1},{3,2},{4,3},{5,4},{6,5},{7,6},{8,7},{9,8},{10,9},{11,1... | collective-permute-start | bytes 49160 | tf_op jit(solution)/shard_map/ppermute | solution.py:16
  111.0 1.3 slice_bitcast_fusion.63
  112.3 2.6 %collective-permute-done.16 = f32[2,2,1024]{2,0,1:T(2,128)S(1)} collective-permute-done((f32[2,2,1024]{2,0,1:T(2,128)S(1)}, f32[2,2,1024]{2,0,1:T(2,128)S(1)}, u32[]{:S(2)}, u32[]{:S(2)}) %collective-permute-start.16) | collective-permute-done | bytes 16416 | tf_op jit(solution)/shard_map/ppermute | solution.py:16
  115.0 0.7 copy-done.15
  115.7 1.0 slice_bitcast_fusion.6
  117.7 0.7 copy-done.2
  118.8 4.5 %collective-permute-start.18 = (f32[2,2,1024]{2,0,1:T(2,128)S(1)}, f32[2,2,1024]{2,0,1:T(2,128)S(1)}, u32[]{:S(2)}, u32[]{:S(2)}) collective-permute-start(f32[2,2,1024]{2,0,1:T(2,128)S(1)} %copy.127), channel_id=1, source_target_pairs={{0,1},{1,2},{2,3},{3,4},{4,5},{5,6},{6,7},{7,8},{8,9},{9,10},{10,1... | collective-permute-start | bytes 49160 | tf_op jit(solution)/shard_map/ppermute | solution.py:16
  123.3 5.4 %collective-permute-start.19 = (f32[2,2,1,512]{3,2,1,0:T(1,128)S(1)}, f32[2,2,1,512]{3,2,1,0:T(1,128)S(1)}, u32[]{:S(2)}, u32[]{:S(2)}) collective-permute-start(f32[2,2,1,512]{3,2,1,0:T(1,128)S(1)} %slice.916), channel_id=1, source_target_pairs={{0,16},{16,32},{32,48},{48,64},{64,80},{80,96},{96,112},{1,17},{17... | collective-permute-start | bytes 24584 | tf_op jit(solution)/shard_map/ppermute | solution.py:16
  128.7 1.3 collective-permute-done.19
  132.5 18.1 %psum.7 = f32[16,512]{1,0:T(8,128)S(1)} all-reduce(f32[16,512]{1,0:T(8,128)S(1)} %add_add_fusion), channel_id=1, replica_groups=mesh['wave'=4,'tx'=8,'ty'=16] {'wave'}, use_global_device_ids=true, to_apply=%region_5.6 | all-reduce | flops 8192 | bytes 65536 | tf_op jit(solution)/shard_map/psum | solution.py:220
  150.6 0.7 fusion.77
  (220 shorter events, 17.7 us)
Async XLA Ops:
  2.0 21.7 %collective-permute-start = (f32[2,2,1024]{2,0,1:T(2,128)S(1)}, f32[2,2,1024]{2,0,1:T(2,128)S(1)}, u32[]{:S(2)}, u32[]{:S(2)}) collective-permute-start(f32[2,2,1024]{2,0,1:T(2,128)S(1)} %reshape.295), channel_id=1, source_target_pairs={{1,0},{2,1},{3,2},{4,3},{5,4},{6,5},{7,6},{8,7},{9,8},{10,9},{11,1... | collective-permute-start | bytes 49160 | tf_op jit(solution)/shard_map/ppermute | solution.py:16
  4.3 2.0 %copy-start.11 = (f32[3,4]{1,0:T(4,128)S(1)}, f32[3,4]{1,0:T(4,128)}, u32[]{:S(2)}) copy-start(f32[3,4]{1,0:T(4,128)} %param.13) | copy-start | bytes 148
  4.3 19.2 %collective-permute-start.1 = (f32[2,2,1,512]{3,2,0,1:T(1,128)S(1)}, f32[2,2,1,512]{3,2,0,1:T(1,128)S(1)}, u32[]{:S(2)}, u32[]{:S(2)}) collective-permute-start(f32[2,2,1,512]{3,2,0,1:T(1,128)S(1)} %slice.789), channel_id=1, source_target_pairs={{16,0},{32,16},{48,32},{64,48},{80,64},{96,80},{112,96},{17,1},{33... | collective-permute-start | bytes 24584 | tf_op jit(solution)/shard_map/ppermute | solution.py:16
  6.9 0.7 copy-start.13
  8.9 79.9 %copy-start.16 = (pred[512]{0:T(512)(128)(4,1)}, pred[512]{0:T(512)(128)(4,1)S(1)}, u32[]{:S(2)}) copy-start(pred[512]{0:T(512)(128)(4,1)S(1)} %broadcast_compare_fusion.3) | copy-start | bytes 1540
  9.0 0.7 copy-start.12
  9.0 2.8 %copy-start.25 = (s32[2]{0:T(128)S(1)}, s32[2]{0:T(128)}, u32[]{:S(2)}) copy-start(s32[2]{0:T(128)} %param.14) | copy-start | bytes 28
  9.6 5.3 %copy-start.9 = (f32[16,512]{1,0:T(8,128)S(1)}, f32[16,512]{1,0:T(8,128)}, u32[]{:S(2)}) copy-start(f32[16,512]{1,0:T(8,128)} %param.12) | copy-start | bytes 98308
  9.6 5.3 %copy-start.10 = (s32[16,512]{1,0:T(8,128)S(1)}, s32[16,512]{1,0:T(8,128)}, u32[]{:S(2)}) copy-start(s32[16,512]{1,0:T(8,128)} %param.11) | copy-start | bytes 98308
  11.1 3.2 %copy-start.21 = (pred[16]{0:T(512)(128)(4,1)}, pred[16]{0:T(512)(128)(4,1)S(1)}, u32[]{:S(2)}) copy-start(pred[16]{0:T(512)(128)(4,1)S(1)} %compare_and_fusion.1) | copy-start | bytes 52
  11.8 90.4 %copy-start.7 = (f32[2,16]{1,0:T(2,128)}, f32[2,16]{1,0:T(2,128)S(1)}, u32[]{:S(2)}) copy-start(f32[2,16]{1,0:T(2,128)S(1)} %compare_convert_fusion) | copy-start | bytes 388
  14.3 0.6 copy-start.23
  23.4 56.8 %copy-start.18 = (pred[512]{0:T(512)(128)(4,1)}, pred[512]{0:T(512)(128)(4,1)S(1)}, u32[]{:S(2)}) copy-start(pred[512]{0:T(512)(128)(4,1)S(1)} %broadcast_compare_fusion.4) | copy-start | bytes 1540
  24.3 10.3 %collective-permute-start.2 = (f32[2,2,1024]{2,0,1:T(2,128)S(1)}, f32[2,2,1024]{2,0,1:T(2,128)S(1)}, u32[]{:S(2)}, u32[]{:S(2)}) collective-permute-start(f32[2,2,1024]{2,0,1:T(2,128)S(1)} %reshape.297), channel_id=1, source_target_pairs={{0,1},{1,2},{2,3},{3,4},{4,5},{5,6},{6,7},{7,8},{8,9},{9,10},{10,1... | collective-permute-start | bytes 49160 | tf_op jit(solution)/shard_map/ppermute | solution.py:16
  27.8 6.8 %collective-permute-start.3 = (f32[2,2,1,512]{3,2,0,1:T(1,128)S(1)}, f32[2,2,1,512]{3,2,0,1:T(1,128)S(1)}, u32[]{:S(2)}, u32[]{:S(2)}) collective-permute-start(f32[2,2,1,512]{3,2,0,1:T(1,128)S(1)} %slice.802), channel_id=1, source_target_pairs={{0,16},{16,32},{32,48},{48,64},{64,80},{80,96},{96,112},{1,17},{17... | collective-permute-start | bytes 24584 | tf_op jit(solution)/shard_map/ppermute | solution.py:16
  35.2 7.0 %collective-permute-start.5 = (f32[2,2,1,512]{3,1,2,0:T(2,128)S(1)}, f32[2,2,1,512]{3,1,2,0:T(2,128)S(1)}, u32[]{:S(2)}, u32[]{:S(2)}) collective-permute-start(f32[2,2,1,512]{3,1,2,0:T(2,128)S(1)} %copy.139), channel_id=1, source_target_pairs={{16,0},{32,16},{48,32},{64,48},{80,64},{96,80},{112,96},{17,1},{33... | collective-permute-start | bytes 24584 | tf_op jit(solution)/shard_map/ppermute | solution.py:16
  37.5 7.9 %collective-permute-start.4 = (f32[2,2,1024]{2,0,1:T(2,128)S(1)}, f32[2,2,1024]{2,0,1:T(2,128)S(1)}, u32[]{:S(2)}, u32[]{:S(2)}) collective-permute-start(f32[2,2,1024]{2,0,1:T(2,128)S(1)} %copy.82), channel_id=1, source_target_pairs={{1,0},{2,1},{3,2},{4,3},{5,4},{6,5},{7,6},{8,7},{9,8},{10,9},{11,1... | collective-permute-start | bytes 49160 | tf_op jit(solution)/shard_map/ppermute | solution.py:16
  46.0 13.5 %collective-permute-start.6 = (f32[2,2,1024]{2,0,1:T(2,128)S(1)}, f32[2,2,1024]{2,0,1:T(2,128)S(1)}, u32[]{:S(2)}, u32[]{:S(2)}) collective-permute-start(f32[2,2,1024]{2,0,1:T(2,128)S(1)} %reshape.301), channel_id=1, source_target_pairs={{0,1},{1,2},{2,3},{3,4},{4,5},{5,6},{6,7},{7,8},{8,9},{9,10},{10,1... | collective-permute-start | bytes 49160 | tf_op jit(solution)/shard_map/ppermute | solution.py:16
  52.7 6.8 %collective-permute-start.7 = (f32[2,2,1,512]{3,2,0,1:T(1,128)S(1)}, f32[2,2,1,512]{3,2,0,1:T(1,128)S(1)}, u32[]{:S(2)}, u32[]{:S(2)}) collective-permute-start(f32[2,2,1,512]{3,2,0,1:T(1,128)S(1)} %slice.832), channel_id=1, source_target_pairs={{0,16},{16,32},{32,48},{48,64},{64,80},{80,96},{96,112},{1,17},{17... | collective-permute-start | bytes 24584 | tf_op jit(solution)/shard_map/ppermute | solution.py:16
  60.1 7.0 %collective-permute-start.9 = (f32[2,2,1,512]{3,2,0,1:T(1,128)S(1)}, f32[2,2,1,512]{3,2,0,1:T(1,128)S(1)}, u32[]{:S(2)}, u32[]{:S(2)}) collective-permute-start(f32[2,2,1,512]{3,2,0,1:T(1,128)S(1)} %slice.847), channel_id=1, source_target_pairs={{16,0},{32,16},{48,32},{64,48},{80,64},{96,80},{112,96},{17,1},{33... | collective-permute-start | bytes 24584 | tf_op jit(solution)/shard_map/ppermute | solution.py:16
  62.4 5.6 %collective-permute-start.8 = (f32[2,2,1024]{2,0,1:T(2,128)S(1)}, f32[2,2,1024]{2,0,1:T(2,128)S(1)}, u32[]{:S(2)}, u32[]{:S(2)}) collective-permute-start(f32[2,2,1024]{2,0,1:T(2,128)S(1)} %copy.95), channel_id=1, source_target_pairs={{1,0},{2,1},{3,2},{4,3},{5,4},{6,5},{7,6},{8,7},{9,8},{10,9},{11,1... | collective-permute-start | bytes 49160 | tf_op jit(solution)/shard_map/ppermute | solution.py:16
  68.7 11.4 %collective-permute-start.10 = (f32[2,2,1024]{2,0,1:T(2,128)S(1)}, f32[2,2,1024]{2,0,1:T(2,128)S(1)}, u32[]{:S(2)}, u32[]{:S(2)}) collective-permute-start(f32[2,2,1024]{2,0,1:T(2,128)S(1)} %reshape.305), channel_id=1, source_target_pairs={{0,1},{1,2},{2,3},{3,4},{4,5},{5,6},{6,7},{7,8},{8,9},{9,10},{10,1... | collective-permute-start | bytes 49160 | tf_op jit(solution)/shard_map/ppermute | solution.py:16
  73.3 6.8 %collective-permute-start.11 = (f32[2,2,1,512]{3,2,0,1:T(1,128)S(1)}, f32[2,2,1,512]{3,2,0,1:T(1,128)S(1)}, u32[]{:S(2)}, u32[]{:S(2)}) collective-permute-start(f32[2,2,1,512]{3,2,0,1:T(1,128)S(1)} %slice.860), channel_id=1, source_target_pairs={{0,16},{16,32},{32,48},{48,64},{64,80},{80,96},{96,112},{1,17},{17... | collective-permute-start | bytes 24584 | tf_op jit(solution)/shard_map/ppermute | solution.py:16
  80.6 7.0 %collective-permute-start.13 = (f32[2,2,1,512]{3,1,2,0:T(2,128)S(1)}, f32[2,2,1,512]{3,1,2,0:T(2,128)S(1)}, u32[]{:S(2)}, u32[]{:S(2)}) collective-permute-start(f32[2,2,1,512]{3,1,2,0:T(2,128)S(1)} %copy.143), channel_id=1, source_target_pairs={{16,0},{32,16},{48,32},{64,48},{80,64},{96,80},{112,96},{17,1},{33... | collective-permute-start | bytes 24584 | tf_op jit(solution)/shard_map/ppermute | solution.py:16
  83.0 5.6 %collective-permute-start.12 = (f32[2,2,1024]{2,0,1:T(2,128)S(1)}, f32[2,2,1024]{2,0,1:T(2,128)S(1)}, u32[]{:S(2)}, u32[]{:S(2)}) collective-permute-start(f32[2,2,1024]{2,0,1:T(2,128)S(1)} %copy.107), channel_id=1, source_target_pairs={{1,0},{2,1},{3,2},{4,3},{5,4},{6,5},{7,6},{8,7},{9,8},{10,9},{11,1... | collective-permute-start | bytes 49160 | tf_op jit(solution)/shard_map/ppermute | solution.py:16
  88.9 0.6 copy-start.1
  88.9 0.6 copy-start.3
  89.8 11.4 %collective-permute-start.14 = (f32[2,2,1024]{2,0,1:T(2,128)S(1)}, f32[2,2,1024]{2,0,1:T(2,128)S(1)}, u32[]{:S(2)}, u32[]{:S(2)}) collective-permute-start(f32[2,2,1024]{2,0,1:T(2,128)S(1)} %reshape.309), channel_id=1, source_target_pairs={{0,1},{1,2},{2,3},{3,4},{4,5},{5,6},{6,7},{7,8},{8,9},{9,10},{10,1... | collective-permute-start | bytes 49160 | tf_op jit(solution)/shard_map/ppermute | solution.py:16
  94.5 6.8 %collective-permute-start.15 = (f32[2,2,1,512]{3,2,0,1:T(1,128)S(1)}, f32[2,2,1,512]{3,2,0,1:T(1,128)S(1)}, u32[]{:S(2)}, u32[]{:S(2)}) collective-permute-start(f32[2,2,1,512]{3,2,0,1:T(1,128)S(1)} %slice.888), channel_id=1, source_target_pairs={{0,16},{16,32},{32,48},{48,64},{64,80},{80,96},{96,112},{1,17},{17... | collective-permute-start | bytes 24584 | tf_op jit(solution)/shard_map/ppermute | solution.py:16
  101.4 0.6 copy-start.19
  103.7 7.4 %collective-permute-start.17 = (f32[2,2,1,512]{3,2,0,1:T(1,128)}, f32[2,2,1,512]{3,2,0,1:T(1,128)}, u32[]{:S(2)}, u32[]{:S(2)}) collective-permute-start(f32[2,2,1,512]{3,2,0,1:T(1,128)} %slice.903), channel_id=1, source_target_pairs={{16,0},{32,16},{48,32},{64,48},{80,64},{96,80},{112,96},{17,1},{33... | collective-permute-start | bytes 24584 | tf_op jit(solution)/shard_map/ppermute | solution.py:16
  109.1 5.8 %collective-permute-start.16 = (f32[2,2,1024]{2,0,1:T(2,128)S(1)}, f32[2,2,1024]{2,0,1:T(2,128)S(1)}, u32[]{:S(2)}, u32[]{:S(2)}) collective-permute-start(f32[2,2,1024]{2,0,1:T(2,128)S(1)} %copy.120), channel_id=1, source_target_pairs={{1,0},{2,1},{3,2},{4,3},{5,4},{6,5},{7,6},{8,7},{9,8},{10,9},{11,1... | collective-permute-start | bytes 49160 | tf_op jit(solution)/shard_map/ppermute | solution.py:16
  115.0 0.7 copy-start.15
  116.6 0.7 copy-start.14
  116.7 0.8 copy-start.5
  116.7 0.9 copy-start.6
  116.7 0.8 copy-start.17
  117.6 0.8 copy-start.2
  117.6 0.9 copy-start.4
  118.8 11.2 %collective-permute-start.18 = (f32[2,2,1024]{2,0,1:T(2,128)S(1)}, f32[2,2,1024]{2,0,1:T(2,128)S(1)}, u32[]{:S(2)}, u32[]{:S(2)}) collective-permute-start(f32[2,2,1024]{2,0,1:T(2,128)S(1)} %copy.127), channel_id=1, source_target_pairs={{0,1},{1,2},{2,3},{3,4},{4,5},{5,6},{6,7},{7,8},{8,9},{9,10},{10,1... | collective-permute-start | bytes 49160 | tf_op jit(solution)/shard_map/ppermute | solution.py:16
  123.3 6.8 %collective-permute-start.19 = (f32[2,2,1,512]{3,2,1,0:T(1,128)S(1)}, f32[2,2,1,512]{3,2,1,0:T(1,128)S(1)}, u32[]{:S(2)}, u32[]{:S(2)}) collective-permute-start(f32[2,2,1,512]{3,2,1,0:T(1,128)S(1)} %slice.916), channel_id=1, source_target_pairs={{0,16},{16,32},{32,48},{48,64},{64,80},{80,96},{96,112},{1,17},{17... | collective-permute-start | bytes 24584 | tf_op jit(solution)/shard_map/ppermute | solution.py:16
  130.2 0.6 copy-start.20
  131.0 0.7 copy-start.8
  131.8 0.7 copy-start
  132.5 18.1 %copy-start.22 = (pred[16]{0:T(512)(128)(4,1)S(1)}, pred[16]{0:T(512)(128)(4,1)}, u32[]{:S(2)}) copy-start(pred[16]{0:T(512)(128)(4,1)} %copy-done.21) | copy-start | bytes 52
  132.5 18.1 %copy-start.24 = (pred[512]{0:T(512)(128)(4,1)S(1)}, pred[512]{0:T(512)(128)(4,1)}, u32[]{:S(2)}) copy-start(pred[512]{0:T(512)(128)(4,1)} %copy-done.23) | copy-start | bytes 1540
where the time goes:
time: 153 us; the launch traced here: 151 us
  starting transfers between devices  71.1 us (46%)
  waiting for transfers between devices  22.2 us (15%)
  local copies, waits for them, and re-layouts  21.2 us (14%)
  blocking collectives  18.1 us (12%)
  other arithmetic  17.2 us (11%)
  between operations  1.69 us (1%)
    ppermute x20, starting transfers between devices, shifted_2(): lax.ppermute(value, axis, [(source, source + steps) for source in range(i...  71.1 us
    ppermute x20, waiting for transfers between devices, shifted_2(): lax.ppermute(value, axis, [(source, source + steps) for source in range(i...  22.2 us
    psum x1, blocking collectives, on_device(): collected = lax.psum(partial_value, 'wave')  18.1 us
    unnamed x55, local copies, waits for them, and re-layouts  8.55 us
    add x1, other arithmetic, coefficients(): decay_map = decay_map + chosen * decay[material_id]  5.68 us
  transfers between devices with their start and end apart: 20, of which 12 were waited for; matrix products, arithmetic and copies ran while one was open for 14% of the time, Pallas kernels for 0%

commit v1 on v0

--- a/solution.py
+++ b/solution.py
@@ -2,6 +2,7 @@
 import jax.numpy as jnp
 from jax import lax
 from jax.sharding import PartitionSpec as P
+from jax.lax import all_gather
 
 NZ = 64
 STEPS = 5
@@ -217,7 +218,11 @@
             * (forward_history[pair_index] - forward_history[pair_index - 1]),
             axis=0,
         )
-    collected = lax.psum(partial_value, "wave")
+
+    def strips_all_bind(link_axis, my_tile):
+        return all_gather(my_tile, link_axis).sum(axis=0)
+
+    collected = strips_all_bind("wave", partial_value)
     density_gradient = contrast * inside_design * collected
     return (density_gradient, electric[None])
 

time: 153 us -> 145 us (0.948)
  blocking collectives: 18.1 us -> 9.32 us
    psum x1 -> x0, blocking collectives: 18.1 us -> none  [on_device(): collected = lax.psum(partial_value, 'wave')]
    all_gather x0 -> x1, blocking collectives: none -> 9.32 us  [strips_all_bind(): return all_gather(my_tile, link_axis).sum(axis=0)]
  transfers between devices with their start and end apart: 20 -> 20, of which waited for: 12 -> 12; matrix products, arithmetic and copies ran while one was open for 14% -> 15% of each run, Pallas kernels for 0% -> 0%
where the time goes in v1:
time: 145 us; the launch traced here: 143 us
  starting transfers between devices  71.1 us (49%)
  waiting for transfers between devices  22.1 us (15%)
  local copies, waits for them, and re-layouts  21.8 us (15%)
  other arithmetic  17.2 us (12%)
  blocking collectives  9.32 us (6%)
  between operations  1.66 us (1%)
    ppermute x20, starting transfers between devices, shifted_2(): lax.ppermute(value, axis, [(source, source + steps) for source in range(i...  71.1 us
    ppermute x20, waiting for transfers between devices, shifted_2(): lax.ppermute(value, axis, [(source, source + steps) for source in range(i...  22.1 us
    all_gather x1, blocking collectives, strips_all_bind(): return all_gather(my_tile, link_axis).sum(axis=0)  9.32 us
    unnamed x55, local copies, waits for them, and re-layouts  9.21 us
    add x1, other arithmetic, coefficients(): decay_map = decay_map + chosen * decay[material_id]  5.68 us
  transfers between devices with their start and end apart: 20, of which 12 were waited for; matrix products, arithmetic and copies ran while one was open for 15% of the time, Pallas kernels for 0%

profile of v1, /device:TPU:212, one launch (start us, length us, event | category | flops | bytes accessed | tf_op | source)
XLA Modules:
  0.0 143.2 jit_solution(14777789026957997822)
XLA Ops:
  0.6 1.2 copy.277
  2.0 2.4 %collective-permute-start = (f32[2,2,1024]{2,0,1:T(2,128)S(1)}, f32[2,2,1024]{2,0,1:T(2,128)S(1)}, u32[]{:S(2)}, u32[]{:S(2)}) collective-permute-start(f32[2,2,1024]{2,0,1:T(2,128)S(1)} %reshape.331), channel_id=1, source_target_pairs={{1,0},{2,1},{3,2},{4,3},{5,4},{6,5},{7,6},{8,7},{9,8},{10,9},{11,1... | collective-permute-start | bytes 49160 | tf_op jit(solution)/shard_map/ppermute | solution.py:17
  4.3 1.9 %collective-permute-start.1 = (f32[2,2,1,512]{3,2,0,1:T(1,128)S(1)}, f32[2,2,1,512]{3,2,0,1:T(1,128)S(1)}, u32[]{:S(2)}, u32[]{:S(2)}) collective-permute-start(f32[2,2,1,512]{3,2,0,1:T(1,128)S(1)} %slice.789), channel_id=1, source_target_pairs={{16,0},{32,16},{48,32},{64,48},{80,64},{96,80},{112,96},{17,1},{33... | collective-permute-start | bytes 24584 | tf_op jit(solution)/shard_map/ppermute | solution.py:17
  9.9 1.2 compare_and_fusion.1
  11.8 2.5 %compare_and_fusion = pred[512]{0:T(512)(128)(4,1)S(1)} fusion(s32[]{:T(128)} %bitcast.5, s32[]{:T(128)} %bitcast.4, s32[]{:T(128)} %bitcast.3, s32[]{:T(128)} %bitcast.2, s32[]{:T(128)S(6)} %mul.416), kind=kLoop, calls=%fused_computation.258 | loop fusion | flops 13824 | bytes 532 | tf_op jit(solution)/shard_map/and | solution.py:107
  14.9 1.9 %fusion.80 = (f32[16,512]{1,0:T(8,128)S(1)}, pred[16,512]{1,0:T(8,128)(4,1)S(1)}, pred[16,512]{1,0:T(8,128)(4,1)S(1)}, pred[16,512]{1,0:T(8,128)(4,1)S(1)}) fusion(f32[16,512]{1,0:T(8,128)S(1)} %copy-done.9, f32[]{:T(128)} %bitcast.9, f32[]{:T(128)} %bitcast.8, f32[]{:T(128)} %bitcast.7, pred[512]{0:T(512)(128)(4,1)S(1)} %compare_and_fusion, ...), kind=kLoop, calls=%fused_computation.208 | loop fusion | flops 106496 | bytes 123420 | tf_op jit(solution)/shard_map/div | solution.py:132
  16.9 0.8 bitcast_multiply_fusion
  17.7 5.7 %select_add_fusion.2 = (f32[16,512]{1,0:T(8,128)S(1)}, f32[16,512]{1,0:T(8,128)S(1)}, f32[16,512]{1,0:T(8,128)S(1)}) fusion(pred[16,512]{1,0:T(8,128)(4,1)S(1)} %get-tuple-element.20, pred[16,512]{1,0:T(8,128)(4,1)S(1)} %get-tuple-element.19, pred[16,512]{1,0:T(8,128)(4,1)S(1)} %get-tuple-element.18, f32[]{:T(128)} %bitcast.30, f32[]{:T(128)} %bitcast.29, ...), kind=kLoop, calls=%fused_computation.212 | loop fusion | flops 122880 | bytes 122916 | tf_op jit(solution)/shard_map/add | solution.py:128
  24.3 3.5 %collective-permute-start.2 = (f32[2,2,1024]{2,0,1:T(2,128)S(1)}, f32[2,2,1024]{2,0,1:T(2,128)S(1)}, u32[]{:S(2)}, u32[]{:S(2)}) collective-permute-start(f32[2,2,1024]{2,0,1:T(2,128)S(1)} %reshape.333), channel_id=1, source_target_pairs={{0,1},{1,2},{2,3},{3,4},{4,5},{5,6},{6,7},{7,8},{8,9},{9,10},{10,1... | collective-permute-start | bytes 49160 | tf_op jit(solution)/shard_map/ppermute | solution.py:17
  27.8 5.5 %collective-permute-start.3 = (f32[2,2,1,512]{3,2,0,1:T(1,128)S(1)}, f32[2,2,1,512]{3,2,0,1:T(1,128)S(1)}, u32[]{:S(2)}, u32[]{:S(2)}) collective-permute-start(f32[2,2,1,512]{3,2,0,1:T(1,128)S(1)} %slice.802), channel_id=1, source_target_pairs={{0,16},{16,32},{32,48},{48,64},{64,80},{80,96},{96,112},{1,17},{17... | collective-permute-start | bytes 24584 | tf_op jit(solution)/shard_map/ppermute | solution.py:17
  33.3 1.3 collective-permute-done.3
  35.2 1.9 %collective-permute-start.5 = (f32[2,2,1,512]{3,1,2,0:T(2,128)S(1)}, f32[2,2,1,512]{3,1,2,0:T(2,128)S(1)}, u32[]{:S(2)}, u32[]{:S(2)}) collective-permute-start(f32[2,2,1,512]{3,1,2,0:T(2,128)S(1)} %copy.204), channel_id=1, source_target_pairs={{16,0},{32,16},{48,32},{64,48},{80,64},{96,80},{112,96},{17,1},{33... | collective-permute-start | bytes 24584 | tf_op jit(solution)/shard_map/ppermute | solution.py:17
  37.5 2.4 %collective-permute-start.4 = (f32[2,2,1024]{2,0,1:T(2,128)S(1)}, f32[2,2,1024]{2,0,1:T(2,128)S(1)}, u32[]{:S(2)}, u32[]{:S(2)}) collective-permute-start(f32[2,2,1024]{2,0,1:T(2,128)S(1)} %copy.147), channel_id=1, source_target_pairs={{1,0},{2,1},{3,2},{4,3},{5,4},{6,5},{7,6},{8,7},{9,8},{10,9},{11,1... | collective-permute-start | bytes 49160 | tf_op jit(solution)/shard_map/ppermute | solution.py:17
  39.8 2.4 %collective-permute-done.5 = f32[2,2,1,512]{3,1,2,0:T(2,128)S(1)} collective-permute-done((f32[2,2,1,512]{3,1,2,0:T(2,128)S(1)}, f32[2,2,1,512]{3,1,2,0:T(2,128)S(1)}, u32[]{:S(2)}, u32[]{:S(2)}) %collective-permute-start.5) | collective-permute-done | bytes 8224 | tf_op jit(solution)/shard_map/ppermute | solution.py:17
  42.3 3.1 %collective-permute-done.4 = f32[2,2,1024]{2,0,1:T(2,128)S(1)} collective-permute-done((f32[2,2,1024]{2,0,1:T(2,128)S(1)}, f32[2,2,1024]{2,0,1:T(2,128)S(1)}, u32[]{:S(2)}, u32[]{:S(2)}) %collective-permute-start.4) | collective-permute-done | bytes 16416 | tf_op jit(solution)/shard_map/ppermute | solution.py:17
  46.0 6.7 %collective-permute-start.6 = (f32[2,2,1024]{2,0,1:T(2,128)S(1)}, f32[2,2,1024]{2,0,1:T(2,128)S(1)}, u32[]{:S(2)}, u32[]{:S(2)}) collective-permute-start(f32[2,2,1024]{2,0,1:T(2,128)S(1)} %reshape.337), channel_id=1, source_target_pairs={{0,1},{1,2},{2,3},{3,4},{4,5},{5,6},{6,7},{7,8},{8,9},{9,10},{10,1... | collective-permute-start | bytes 49160 | tf_op jit(solution)/shard_map/ppermute | solution.py:17
  52.7 5.4 %collective-permute-start.7 = (f32[2,2,1,512]{3,2,0,1:T(1,128)S(1)}, f32[2,2,1,512]{3,2,0,1:T(1,128)S(1)}, u32[]{:S(2)}, u32[]{:S(2)}) collective-permute-start(f32[2,2,1,512]{3,2,0,1:T(1,128)S(1)} %slice.832), channel_id=1, source_target_pairs={{0,16},{16,32},{32,48},{48,64},{64,80},{80,96},{96,112},{1,17},{17... | collective-permute-start | bytes 24584 | tf_op jit(solution)/shard_map/ppermute | solution.py:17
  58.1 1.3 collective-permute-done.7
  60.1 1.9 %collective-permute-start.9 = (f32[2,2,1,512]{3,2,0,1:T(1,128)S(1)}, f32[2,2,1,512]{3,2,0,1:T(1,128)S(1)}, u32[]{:S(2)}, u32[]{:S(2)}) collective-permute-start(f32[2,2,1,512]{3,2,0,1:T(1,128)S(1)} %slice.847), channel_id=1, source_target_pairs={{16,0},{32,16},{48,32},{64,48},{80,64},{96,80},{112,96},{17,1},{33... | collective-permute-start | bytes 24584 | tf_op jit(solution)/shard_map/ppermute | solution.py:17
  62.4 1.9 %collective-permute-start.8 = (f32[2,2,1024]{2,0,1:T(2,128)S(1)}, f32[2,2,1024]{2,0,1:T(2,128)S(1)}, u32[]{:S(2)}, u32[]{:S(2)}) collective-permute-start(f32[2,2,1024]{2,0,1:T(2,128)S(1)} %copy.160), channel_id=1, source_target_pairs={{1,0},{2,1},{3,2},{4,3},{5,4},{6,5},{7,6},{8,7},{9,8},{10,9},{11,1... | collective-permute-start | bytes 49160 | tf_op jit(solution)/shard_map/ppermute | solution.py:17
  64.3 2.8 %collective-permute-done.9 = f32[2,2,1,512]{3,2,0,1:T(1,128)S(1)} collective-permute-done((f32[2,2,1,512]{3,2,0,1:T(1,128)S(1)}, f32[2,2,1,512]{3,2,0,1:T(1,128)S(1)}, u32[]{:S(2)}, u32[]{:S(2)}) %collective-permute-start.9) | collective-permute-done | bytes 8224 | tf_op jit(solution)/shard_map/ppermute | solution.py:17
  67.1 0.9 collective-permute-done.8
  68.6 4.6 %collective-permute-start.10 = (f32[2,2,1024]{2,0,1:T(2,128)S(1)}, f32[2,2,1024]{2,0,1:T(2,128)S(1)}, u32[]{:S(2)}, u32[]{:S(2)}) collective-permute-start(f32[2,2,1024]{2,0,1:T(2,128)S(1)} %reshape.341), channel_id=1, source_target_pairs={{0,1},{1,2},{2,3},{3,4},{4,5},{5,6},{6,7},{7,8},{8,9},{9,10},{10,1... | collective-permute-start | bytes 49160 | tf_op jit(solution)/shard_map/ppermute | solution.py:17
  73.3 5.4 %collective-permute-start.11 = (f32[2,2,1,512]{3,2,0,1:T(1,128)S(1)}, f32[2,2,1,512]{3,2,0,1:T(1,128)S(1)}, u32[]{:S(2)}, u32[]{:S(2)}) collective-permute-start(f32[2,2,1,512]{3,2,0,1:T(1,128)S(1)} %slice.860), channel_id=1, source_target_pairs={{0,16},{16,32},{32,48},{48,64},{64,80},{80,96},{96,112},{1,17},{17... | collective-permute-start | bytes 24584 | tf_op jit(solution)/shard_map/ppermute | solution.py:17
  78.7 1.3 collective-permute-done.11
  80.6 1.9 %collective-permute-start.13 = (f32[2,2,1,512]{3,1,2,0:T(2,128)S(1)}, f32[2,2,1,512]{3,1,2,0:T(2,128)S(1)}, u32[]{:S(2)}, u32[]{:S(2)}) collective-permute-start(f32[2,2,1,512]{3,1,2,0:T(2,128)S(1)} %copy.208), channel_id=1, source_target_pairs={{16,0},{32,16},{48,32},{64,48},{80,64},{96,80},{112,96},{17,1},{33... | collective-permute-start | bytes 24584 | tf_op jit(solution)/shard_map/ppermute | solution.py:17
  83.0 1.9 %collective-permute-start.12 = (f32[2,2,1024]{2,0,1:T(2,128)S(1)}, f32[2,2,1024]{2,0,1:T(2,128)S(1)}, u32[]{:S(2)}, u32[]{:S(2)}) collective-permute-start(f32[2,2,1024]{2,0,1:T(2,128)S(1)} %copy.172), channel_id=1, source_target_pairs={{1,0},{2,1},{3,2},{4,3},{5,4},{6,5},{7,6},{8,7},{9,8},{10,9},{11,1... | collective-permute-start | bytes 49160 | tf_op jit(solution)/shard_map/ppermute | solution.py:17
  84.9 2.7 %collective-permute-done.13 = f32[2,2,1,512]{3,1,2,0:T(2,128)S(1)} collective-permute-done((f32[2,2,1,512]{3,1,2,0:T(2,128)S(1)}, f32[2,2,1,512]{3,1,2,0:T(2,128)S(1)}, u32[]{:S(2)}, u32[]{:S(2)}) %collective-permute-start.13) | collective-permute-done | bytes 8224 | tf_op jit(solution)/shard_map/ppermute | solution.py:17
  87.6 1.0 collective-permute-done.12
  89.8 4.6 %collective-permute-start.14 = (f32[2,2,1024]{2,0,1:T(2,128)S(1)}, f32[2,2,1024]{2,0,1:T(2,128)S(1)}, u32[]{:S(2)}, u32[]{:S(2)}) collective-permute-start(f32[2,2,1024]{2,0,1:T(2,128)S(1)} %reshape.345), channel_id=1, source_target_pairs={{0,1},{1,2},{2,3},{3,4},{4,5},{5,6},{6,7},{7,8},{8,9},{9,10},{10,1... | collective-permute-start | bytes 49160 | tf_op jit(solution)/shard_map/ppermute | solution.py:17
  94.5 5.4 %collective-permute-start.15 = (f32[2,2,1,512]{3,2,0,1:T(1,128)S(1)}, f32[2,2,1,512]{3,2,0,1:T(1,128)S(1)}, u32[]{:S(2)}, u32[]{:S(2)}) collective-permute-start(f32[2,2,1,512]{3,2,0,1:T(1,128)S(1)} %slice.888), channel_id=1, source_target_pairs={{0,16},{16,32},{32,48},{48,64},{64,80},{80,96},{96,112},{1,17},{17... | collective-permute-start | bytes 24584 | tf_op jit(solution)/shard_map/ppermute | solution.py:17
  99.9 1.3 collective-permute-done.15
  102.9 0.7 slice_bitcast_fusion.4
  103.7 1.9 %collective-permute-start.17 = (f32[2,2,1,512]{3,2,0,1:T(1,128)}, f32[2,2,1,512]{3,2,0,1:T(1,128)}, u32[]{:S(2)}, u32[]{:S(2)}) collective-permute-start(f32[2,2,1,512]{3,2,0,1:T(1,128)} %slice.903), channel_id=1, source_target_pairs={{16,0},{32,16},{48,32},{64,48},{80,64},{96,80},{112,96},{17,1},{33... | collective-permute-start | bytes 24584 | tf_op jit(solution)/shard_map/ppermute | solution.py:17
  106.8 0.7 slice.899
  107.5 0.7 slice.901
  108.2 0.8 reshape.347
  109.1 1.9 %collective-permute-start.16 = (f32[2,2,1024]{2,0,1:T(2,128)S(1)}, f32[2,2,1024]{2,0,1:T(2,128)S(1)}, u32[]{:S(2)}, u32[]{:S(2)}) collective-permute-start(f32[2,2,1024]{2,0,1:T(2,128)S(1)} %copy.185), channel_id=1, source_target_pairs={{1,0},{2,1},{3,2},{4,3},{5,4},{6,5},{7,6},{8,7},{9,8},{10,9},{11,1... | collective-permute-start | bytes 49160 | tf_op jit(solution)/shard_map/ppermute | solution.py:17
  111.0 1.3 slice_bitcast_fusion.63
  112.3 2.6 %collective-permute-done.16 = f32[2,2,1024]{2,0,1:T(2,128)S(1)} collective-permute-done((f32[2,2,1024]{2,0,1:T(2,128)S(1)}, f32[2,2,1024]{2,0,1:T(2,128)S(1)}, u32[]{:S(2)}, u32[]{:S(2)}) %collective-permute-start.16) | collective-permute-done | bytes 16416 | tf_op jit(solution)/shard_map/ppermute | solution.py:17
  115.0 0.7 copy-done.15
  115.6 1.0 slice_bitcast_fusion.6
  117.7 0.7 copy-done.2
  118.8 4.5 %collective-permute-start.18 = (f32[2,2,1024]{2,0,1:T(2,128)S(1)}, f32[2,2,1024]{2,0,1:T(2,128)S(1)}, u32[]{:S(2)}, u32[]{:S(2)}) collective-permute-start(f32[2,2,1024]{2,0,1:T(2,128)S(1)} %copy.192), channel_id=1, source_target_pairs={{0,1},{1,2},{2,3},{3,4},{4,5},{5,6},{6,7},{7,8},{8,9},{9,10},{10,1... | collective-permute-start | bytes 49160 | tf_op jit(solution)/shard_map/ppermute | solution.py:17
  123.2 5.4 %collective-permute-start.19 = (f32[2,2,1,512]{3,2,1,0:T(1,128)S(1)}, f32[2,2,1,512]{3,2,1,0:T(1,128)S(1)}, u32[]{:S(2)}, u32[]{:S(2)}) collective-permute-start(f32[2,2,1,512]{3,2,1,0:T(1,128)S(1)} %slice.916), channel_id=1, source_target_pairs={{0,16},{16,32},{32,48},{48,64},{64,80},{80,96},{96,112},{1,17},{17... | collective-permute-start | bytes 24584 | tf_op jit(solution)/shard_map/ppermute | solution.py:17
  128.7 1.3 collective-permute-done.19
  132.5 9.3 %all-gather = f32[64,512]{1,0:T(8,128)S(1)} all-gather(f32[16,512]{1,0:T(8,128)S(1)} %add_add_fusion), channel_id=2, replica_groups=mesh['wave'=4,'tx'=8,'ty'=16] {'wave'}, dimensions={0}, use_global_device_ids=true | all-gather | bytes 163840 | tf_op jit(solution)/shard_map/all_gather | solution.py:223
  142.5 0.7 fusion.77
  (221 shorter events, 18.3 us)
Async XLA Ops:
  2.0 21.7 %collective-permute-start = (f32[2,2,1024]{2,0,1:T(2,128)S(1)}, f32[2,2,1024]{2,0,1:T(2,128)S(1)}, u32[]{:S(2)}, u32[]{:S(2)}) collective-permute-start(f32[2,2,1024]{2,0,1:T(2,128)S(1)} %reshape.331), channel_id=1, source_target_pairs={{1,0},{2,1},{3,2},{4,3},{5,4},{6,5},{7,6},{8,7},{9,8},{10,9},{11,1... | collective-permute-start | bytes 49160 | tf_op jit(solution)/shard_map/ppermute | solution.py:17
  4.3 2.0 %copy-start.11 = (f32[3,4]{1,0:T(4,128)S(1)}, f32[3,4]{1,0:T(4,128)}, u32[]{:S(2)}) copy-start(f32[3,4]{1,0:T(4,128)} %param.13) | copy-start | bytes 148
  4.3 19.2 %collective-permute-start.1 = (f32[2,2,1,512]{3,2,0,1:T(1,128)S(1)}, f32[2,2,1,512]{3,2,0,1:T(1,128)S(1)}, u32[]{:S(2)}, u32[]{:S(2)}) collective-permute-start(f32[2,2,1,512]{3,2,0,1:T(1,128)S(1)} %slice.789), channel_id=1, source_target_pairs={{16,0},{32,16},{48,32},{64,48},{80,64},{96,80},{112,96},{17,1},{33... | collective-permute-start | bytes 24584 | tf_op jit(solution)/shard_map/ppermute | solution.py:17
  6.9 0.7 copy-start.13
  8.9 79.9 %copy-start.16 = (pred[512]{0:T(512)(128)(4,1)}, pred[512]{0:T(512)(128)(4,1)S(1)}, u32[]{:S(2)}) copy-start(pred[512]{0:T(512)(128)(4,1)S(1)} %broadcast_compare_fusion.3) | copy-start | bytes 1540
  9.0 0.7 copy-start.12
  9.0 2.8 %copy-start.25 = (s32[2]{0:T(128)S(1)}, s32[2]{0:T(128)}, u32[]{:S(2)}) copy-start(s32[2]{0:T(128)} %param.14) | copy-start | bytes 28
  9.6 5.3 %copy-start.9 = (f32[16,512]{1,0:T(8,128)S(1)}, f32[16,512]{1,0:T(8,128)}, u32[]{:S(2)}) copy-start(f32[16,512]{1,0:T(8,128)} %param.12) | copy-start | bytes 98308
  9.6 5.3 %copy-start.10 = (s32[16,512]{1,0:T(8,128)S(1)}, s32[16,512]{1,0:T(8,128)}, u32[]{:S(2)}) copy-start(s32[16,512]{1,0:T(8,128)} %param.11) | copy-start | bytes 98308
  11.1 3.2 %copy-start.21 = (pred[16]{0:T(512)(128)(4,1)}, pred[16]{0:T(512)(128)(4,1)S(1)}, u32[]{:S(2)}) copy-start(pred[16]{0:T(512)(128)(4,1)S(1)} %compare_and_fusion.1) | copy-start | bytes 52
  11.8 90.4 %copy-start.7 = (f32[2,16]{1,0:T(2,128)}, f32[2,16]{1,0:T(2,128)S(1)}, u32[]{:S(2)}) copy-start(f32[2,16]{1,0:T(2,128)S(1)} %compare_convert_fusion) | copy-start | bytes 388
  14.3 0.6 copy-start.23
  23.4 56.8 %copy-start.18 = (pred[512]{0:T(512)(128)(4,1)}, pred[512]{0:T(512)(128)(4,1)S(1)}, u32[]{:S(2)}) copy-start(pred[512]{0:T(512)(128)(4,1)S(1)} %broadcast_compare_fusion.4) | copy-start | bytes 1540
  24.3 10.3 %collective-permute-start.2 = (f32[2,2,1024]{2,0,1:T(2,128)S(1)}, f32[2,2,1024]{2,0,1:T(2,128)S(1)}, u32[]{:S(2)}, u32[]{:S(2)}) collective-permute-start(f32[2,2,1024]{2,0,1:T(2,128)S(1)} %reshape.333), channel_id=1, source_target_pairs={{0,1},{1,2},{2,3},{3,4},{4,5},{5,6},{6,7},{7,8},{8,9},{9,10},{10,1... | collective-permute-start | bytes 49160 | tf_op jit(solution)/shard_map/ppermute | solution.py:17
  27.8 6.8 %collective-permute-start.3 = (f32[2,2,1,512]{3,2,0,1:T(1,128)S(1)}, f32[2,2,1,512]{3,2,0,1:T(1,128)S(1)}, u32[]{:S(2)}, u32[]{:S(2)}) collective-permute-start(f32[2,2,1,512]{3,2,0,1:T(1,128)S(1)} %slice.802), channel_id=1, source_target_pairs={{0,16},{16,32},{32,48},{48,64},{64,80},{80,96},{96,112},{1,17},{17... | collective-permute-start | bytes 24584 | tf_op jit(solution)/shard_map/ppermute | solution.py:17
  35.2 7.0 %collective-permute-start.5 = (f32[2,2,1,512]{3,1,2,0:T(2,128)S(1)}, f32[2,2,1,512]{3,1,2,0:T(2,128)S(1)}, u32[]{:S(2)}, u32[]{:S(2)}) collective-permute-start(f32[2,2,1,512]{3,1,2,0:T(2,128)S(1)} %copy.204), channel_id=1, source_target_pairs={{16,0},{32,16},{48,32},{64,48},{80,64},{96,80},{112,96},{17,1},{33... | collective-permute-start | bytes 24584 | tf_op jit(solution)/shard_map/ppermute | solution.py:17
  37.5 7.9 %collective-permute-start.4 = (f32[2,2,1024]{2,0,1:T(2,128)S(1)}, f32[2,2,1024]{2,0,1:T(2,128)S(1)}, u32[]{:S(2)}, u32[]{:S(2)}) collective-permute-start(f32[2,2,1024]{2,0,1:T(2,128)S(1)} %copy.147), channel_id=1, source_target_pairs={{1,0},{2,1},{3,2},{4,3},{5,4},{6,5},{7,6},{8,7},{9,8},{10,9},{11,1... | collective-permute-start | bytes 49160 | tf_op jit(solution)/shard_map/ppermute | solution.py:17
  46.0 13.5 %collective-permute-start.6 = (f32[2,2,1024]{2,0,1:T(2,128)S(1)}, f32[2,2,1024]{2,0,1:T(2,128)S(1)}, u32[]{:S(2)}, u32[]{:S(2)}) collective-permute-start(f32[2,2,1024]{2,0,1:T(2,128)S(1)} %reshape.337), channel_id=1, source_target_pairs={{0,1},{1,2},{2,3},{3,4},{4,5},{5,6},{6,7},{7,8},{8,9},{9,10},{10,1... | collective-permute-start | bytes 49160 | tf_op jit(solution)/shard_map/ppermute | solution.py:17
  52.7 6.8 %collective-permute-start.7 = (f32[2,2,1,512]{3,2,0,1:T(1,128)S(1)}, f32[2,2,1,512]{3,2,0,1:T(1,128)S(1)}, u32[]{:S(2)}, u32[]{:S(2)}) collective-permute-start(f32[2,2,1,512]{3,2,0,1:T(1,128)S(1)} %slice.832), channel_id=1, source_target_pairs={{0,16},{16,32},{32,48},{48,64},{64,80},{80,96},{96,112},{1,17},{17... | collective-permute-start | bytes 24584 | tf_op jit(solution)/shard_map/ppermute | solution.py:17
  60.1 7.0 %collective-permute-start.9 = (f32[2,2,1,512]{3,2,0,1:T(1,128)S(1)}, f32[2,2,1,512]{3,2,0,1:T(1,128)S(1)}, u32[]{:S(2)}, u32[]{:S(2)}) collective-permute-start(f32[2,2,1,512]{3,2,0,1:T(1,128)S(1)} %slice.847), channel_id=1, source_target_pairs={{16,0},{32,16},{48,32},{64,48},{80,64},{96,80},{112,96},{17,1},{33... | collective-permute-start | bytes 24584 | tf_op jit(solution)/shard_map/ppermute | solution.py:17
  62.4 5.6 %collective-permute-start.8 = (f32[2,2,1024]{2,0,1:T(2,128)S(1)}, f32[2,2,1024]{2,0,1:T(2,128)S(1)}, u32[]{:S(2)}, u32[]{:S(2)}) collective-permute-start(f32[2,2,1024]{2,0,1:T(2,128)S(1)} %copy.160), channel_id=1, source_target_pairs={{1,0},{2,1},{3,2},{4,3},{5,4},{6,5},{7,6},{8,7},{9,8},{10,9},{11,1... | collective-permute-start | bytes 49160 | tf_op jit(solution)/shard_map/ppermute | solution.py:17
  68.6 11.4 %collective-permute-start.10 = (f32[2,2,1024]{2,0,1:T(2,128)S(1)}, f32[2,2,1024]{2,0,1:T(2,128)S(1)}, u32[]{:S(2)}, u32[]{:S(2)}) collective-permute-start(f32[2,2,1024]{2,0,1:T(2,128)S(1)} %reshape.341), channel_id=1, source_target_pairs={{0,1},{1,2},{2,3},{3,4},{4,5},{5,6},{6,7},{7,8},{8,9},{9,10},{10,1... | collective-permute-start | bytes 49160 | tf_op jit(solution)/shard_map/ppermute | solution.py:17
  73.3 6.8 %collective-permute-start.11 = (f32[2,2,1,512]{3,2,0,1:T(1,128)S(1)}, f32[2,2,1,512]{3,2,0,1:T(1,128)S(1)}, u32[]{:S(2)}, u32[]{:S(2)}) collective-permute-start(f32[2,2,1,512]{3,2,0,1:T(1,128)S(1)} %slice.860), channel_id=1, source_target_pairs={{0,16},{16,32},{32,48},{48,64},{64,80},{80,96},{96,112},{1,17},{17... | collective-permute-start | bytes 24584 | tf_op jit(solution)/shard_map/ppermute | solution.py:17
  80.6 7.0 %collective-permute-start.13 = (f32[2,2,1,512]{3,1,2,0:T(2,128)S(1)}, f32[2,2,1,512]{3,1,2,0:T(2,128)S(1)}, u32[]{:S(2)}, u32[]{:S(2)}) collective-permute-start(f32[2,2,1,512]{3,1,2,0:T(2,128)S(1)} %copy.208), channel_id=1, source_target_pairs={{16,0},{32,16},{48,32},{64,48},{80,64},{96,80},{112,96},{17,1},{33... | collective-permute-start | bytes 24584 | tf_op jit(solution)/shard_map/ppermute | solution.py:17
  83.0 5.6 %collective-permute-start.12 = (f32[2,2,1024]{2,0,1:T(2,128)S(1)}, f32[2,2,1024]{2,0,1:T(2,128)S(1)}, u32[]{:S(2)}, u32[]{:S(2)}) collective-permute-start(f32[2,2,1024]{2,0,1:T(2,128)S(1)} %copy.172), channel_id=1, source_target_pairs={{1,0},{2,1},{3,2},{4,3},{5,4},{6,5},{7,6},{8,7},{9,8},{10,9},{11,1... | collective-permute-start | bytes 49160 | tf_op jit(solution)/shard_map/ppermute | solution.py:17
  88.9 0.6 copy-start.1
  88.9 0.6 copy-start.3
  89.8 11.4 %collective-permute-start.14 = (f32[2,2,1024]{2,0,1:T(2,128)S(1)}, f32[2,2,1024]{2,0,1:T(2,128)S(1)}, u32[]{:S(2)}, u32[]{:S(2)}) collective-permute-start(f32[2,2,1024]{2,0,1:T(2,128)S(1)} %reshape.345), channel_id=1, source_target_pairs={{0,1},{1,2},{2,3},{3,4},{4,5},{5,6},{6,7},{7,8},{8,9},{9,10},{10,1... | collective-permute-start | bytes 49160 | tf_op jit(solution)/shard_map/ppermute | solution.py:17
  94.5 6.8 %collective-permute-start.15 = (f32[2,2,1,512]{3,2,0,1:T(1,128)S(1)}, f32[2,2,1,512]{3,2,0,1:T(1,128)S(1)}, u32[]{:S(2)}, u32[]{:S(2)}) collective-permute-start(f32[2,2,1,512]{3,2,0,1:T(1,128)S(1)} %slice.888), channel_id=1, source_target_pairs={{0,16},{16,32},{32,48},{48,64},{64,80},{80,96},{96,112},{1,17},{17... | collective-permute-start | bytes 24584 | tf_op jit(solution)/shard_map/ppermute | solution.py:17
  101.4 0.6 copy-start.19
  103.7 7.4 %collective-permute-start.17 = (f32[2,2,1,512]{3,2,0,1:T(1,128)}, f32[2,2,1,512]{3,2,0,1:T(1,128)}, u32[]{:S(2)}, u32[]{:S(2)}) collective-permute-start(f32[2,2,1,512]{3,2,0,1:T(1,128)} %slice.903), channel_id=1, source_target_pairs={{16,0},{32,16},{48,32},{64,48},{80,64},{96,80},{112,96},{17,1},{33... | collective-permute-start | bytes 24584 | tf_op jit(solution)/shard_map/ppermute | solution.py:17
  109.1 5.8 %collective-permute-start.16 = (f32[2,2,1024]{2,0,1:T(2,128)S(1)}, f32[2,2,1024]{2,0,1:T(2,128)S(1)}, u32[]{:S(2)}, u32[]{:S(2)}) collective-permute-start(f32[2,2,1024]{2,0,1:T(2,128)S(1)} %copy.185), channel_id=1, source_target_pairs={{1,0},{2,1},{3,2},{4,3},{5,4},{6,5},{7,6},{8,7},{9,8},{10,9},{11,1... | collective-permute-start | bytes 49160 | tf_op jit(solution)/shard_map/ppermute | solution.py:17
  115.0 0.7 copy-start.15
  116.6 0.7 copy-start.14
  116.7 0.8 copy-start.5
  116.7 0.9 copy-start.6
  116.7 0.8 copy-start.17
  117.6 0.8 copy-start.2
  117.6 0.9 copy-start.4
  118.8 11.2 %collective-permute-start.18 = (f32[2,2,1024]{2,0,1:T(2,128)S(1)}, f32[2,2,1024]{2,0,1:T(2,128)S(1)}, u32[]{:S(2)}, u32[]{:S(2)}) collective-permute-start(f32[2,2,1024]{2,0,1:T(2,128)S(1)} %copy.192), channel_id=1, source_target_pairs={{0,1},{1,2},{2,3},{3,4},{4,5},{5,6},{6,7},{7,8},{8,9},{9,10},{10,1... | collective-permute-start | bytes 49160 | tf_op jit(solution)/shard_map/ppermute | solution.py:17
  123.2 6.8 %collective-permute-start.19 = (f32[2,2,1,512]{3,2,1,0:T(1,128)S(1)}, f32[2,2,1,512]{3,2,1,0:T(1,128)S(1)}, u32[]{:S(2)}, u32[]{:S(2)}) collective-permute-start(f32[2,2,1,512]{3,2,1,0:T(1,128)S(1)} %slice.916), channel_id=1, source_target_pairs={{0,16},{16,32},{32,48},{48,64},{64,80},{80,96},{96,112},{1,17},{17... | collective-permute-start | bytes 24584 | tf_op jit(solution)/shard_map/ppermute | solution.py:17
  130.2 0.6 copy-start.20
  130.9 0.7 copy-start.8
  131.8 0.7 copy-start
  141.8 0.7 copy-start.22
  141.8 0.7 copy-start.24
